TPU v7x, 32 devices: a whole 2x2x4 slice. The times are simulated.
32 devices in a mesh: groups: 2 (over x), row: 16 (over z, y, core).
Axes of the slice: x: 2, y: 2, z: 4, core: 2. Of those that a mesh axis runs over, the one named last changes fastest.
Arguments:
- features: bfloat16 [128, 64, 512], P(('groups', 'row')), parts along dimension 0, may hold values from -6 to 6
- cotangent: bfloat16 [128, 64, 512], P(('groups', 'row')), parts along dimension 0, may hold values from -6 to 6
- depth_weight: bfloat16 [49, 512], P(None, 'row'), may hold values from -0.875 to 0.875
- depth_bias: bfloat16 [512], P('row'), may hold values from -3 to 3
- norm_gain: bfloat16 [512], P('row'), may hold values from 0.25 to 1.75
- norm_shift: bfloat16 [512], P('row'), may hold values from -3 to 3
- up_weight: bfloat16 [512, 2048], P('row'), may hold values from -0.25 to 0.25
- up_bias: bfloat16 [2048], P('row'), may hold values from -3 to 3
- down_weight: bfloat16 [2048, 512], P('row'), may hold values from -0.125 to 0.125
- down_bias: bfloat16 [512], P('row'), may hold values from -3 to 3
Outputs:
- block_out: bfloat16 [128, 64, 512], P(('groups', 'row')), parts along dimension 0
- grad_features: bfloat16 [128, 64, 512], P(('groups', 'row')), parts along dimension 0
- grad_up_weight: float32 [1024, 2048], P(('groups', 'row')), parts along dimension 0
- grad_down_weight: float32 [4096, 512], P(('groups', 'row')), parts along dimension 0
- grad_depth_weight: float32 [98, 512], P('groups', 'row'), parts along dimension 0
- grad_depth_bias: float32 [1024], P(('groups', 'row')), parts along dimension 0
- grad_norm_gain: float32 [1024], P(('groups', 'row')), parts along dimension 0
- grad_norm_shift: float32 [1024], P(('groups', 'row')), parts along dimension 0
- grad_up_bias: float32 [4096], P(('groups', 'row')), parts along dimension 0
- grad_down_bias: float32 [1024], P(('groups', 'row')), parts along dimension 0
There are 2 independent parts, one for each index of `groups`. A program takes and returns all parts, laid end to end along the dimension named above; an argument that names none is the same for every part. Nothing has to cross between parts.
All inputs are finite; a program needn't handle non-finite values.
Results may differ from a plain program's by a relative error of at most 0.0055.
Values may be sent and summed in bfloat16 or wider, within the bound.
A program may use at most 64 MiB of HBM per device.

v0:
```python
import math
import jax
import jax.numpy as jnp
from jax import lax
from jax.sharding import PartitionSpec as P

eps = 1e-06


def with_halo(block, sides, width):
    for axis, dim in sides:
        count = lax.axis_size(axis)
        forward = [(i, i + 1) for i in range(count - 1)]
        backward = [(target, source) for source, target in forward]
        low = lax.ppermute(
            lax.slice_in_dim(block, block.shape[dim] - width, None, axis=dim), axis, forward
        )
        high = lax.ppermute(lax.slice_in_dim(block, 0, width, axis=dim), axis, backward)
        block = jnp.concatenate([low, block, high], axis=dim)
    return block


def gelu_value(value):
    return 0.5 * value * (1.0 + lax.erf(value * (1.0 / math.sqrt(2.0))))


def gelu_slope(value):
    cumulative = 0.5 * (1.0 + lax.erf(value * (1.0 / math.sqrt(2.0))))
    density = jnp.exp(-0.5 * value * value) * (1.0 / math.sqrt(2.0 * math.pi))
    return cumulative + value * density


def depth_conv(padded, kernel, height, width):
    total = jnp.zeros((height, width, kernel.shape[1]), jnp.float32)
    for first in range(7):
        for second in range(7):
            total = (
                total
                + padded[first : first + height, second : second + width, :]
                * kernel[first * 7 + second]
            )
    return total


def depth_conv_back(padded, kernel, height, width):
    total = jnp.zeros((height, width, kernel.shape[1]), jnp.float32)
    for first in range(7):
        for second in range(7):
            total = (
                total
                + padded[6 - first : 6 - first + height, 6 - second : 6 - second + width, :]
                * kernel[first * 7 + second]
            )
    return total


def per_device(
    features,
    cotangent,
    depth_weight,
    depth_bias,
    norm_gain,
    norm_shift,
    up_weight,
    up_bias,
    down_weight,
    down_bias,
):
    height, width, chans = features.shape
    devices = lax.axis_size("row")
    cells = height * width
    scale = 1.0 / math.sqrt(cells * devices)
    kernel, conv_bias, gain, shift, bias_down, bias_up = (
        lax.all_gather(depth_weight, "row", axis=1, tiled=True),
        lax.all_gather(depth_bias, "row", axis=0, tiled=True),
        lax.all_gather(norm_gain, "row", axis=0, tiled=True),
        lax.all_gather(norm_shift, "row", axis=0, tiled=True),
        lax.all_gather(down_bias, "row", axis=0, tiled=True),
        lax.all_gather(up_bias, "row", axis=0, tiled=True),
    )
    kernel = kernel.astype(jnp.float32)
    gain = gain.astype(jnp.float32)
    rimmed = with_halo(features, (("row", 0),), 3)
    padded = jnp.pad(rimmed.astype(jnp.float32), ((0, 0), (3, 3), (0, 0)))
    conv = depth_conv(padded, kernel, height, width) + conv_bias.astype(jnp.float32)
    mean_val = jnp.mean(conv, axis=2, keepdims=True)
    centered = conv - mean_val
    var_val = jnp.mean(centered * centered, axis=2, keepdims=True)
    inv = lax.rsqrt(var_val + eps)
    normed = centered * inv
    normal_out = (normed * gain + shift.astype(jnp.float32)).astype(jnp.bfloat16)
    flat_norm = normal_out.reshape(cells, chans)
    flat_cot = cotangent.reshape(cells, chans)
    columns = flat_norm
    hidden = jnp.dot(
        columns,
        lax.all_gather(up_weight, "row", axis=0, tiled=True),
        preferred_element_type=jnp.float32,
    ) + bias_up.astype(jnp.float32)
    act = gelu_value(hidden).astype(jnp.bfloat16)
    columns = act
    mixed = jnp.dot(
        columns,
        lax.all_gather(down_weight, "row", axis=0, tiled=True),
        preferred_element_type=jnp.float32,
    )
    block_out = (
        features.astype(jnp.float32)
        + (mixed + bias_down.astype(jnp.float32)).reshape(height, width, chans)
    ).astype(jnp.bfloat16)
    down_full = (
        lax.dot_general(act, flat_cot, (((0,), (0,)), ((), ())), preferred_element_type=jnp.float32)
        * scale
    )
    grad_down_weight = lax.psum_scatter(down_full, "row", scatter_dimension=0, tiled=True)
    dact = lax.dot_general(
        flat_cot,
        lax.all_gather(down_weight, "row", axis=0, tiled=True),
        (((1,), (1,)), ((), ())),
        preferred_element_type=jnp.float32,
    )
    dhidden = (dact * gelu_slope(hidden)).astype(jnp.bfloat16)
    columns = flat_norm
    grad_up_weight = lax.psum_scatter(
        lax.dot_general(
            columns, dhidden, (((0,), (0,)), ((), ())), preferred_element_type=jnp.float32
        )
        * scale,
        "row",
        scatter_dimension=0,
        tiled=True,
    )
    dnorm = lax.dot_general(
        dhidden,
        lax.all_gather(up_weight, "row", axis=0, tiled=True),
        (((1,), (1,)), ((), ())),
        preferred_element_type=jnp.float32,
    )
    dnorm = dnorm.reshape(height, width, chans)
    down_bias_term = jnp.sum(flat_cot.astype(jnp.float32), axis=0) * scale
    up_bias_term = jnp.sum(dhidden.astype(jnp.float32), axis=0) * scale
    gain_term = jnp.sum(dnorm * normed, axis=(0, 1)) * scale
    shift_term = jnp.sum(dnorm, axis=(0, 1)) * scale
    grad_down_bias, grad_up_bias, grad_norm_gain, grad_norm_shift = (
        lax.psum_scatter(down_bias_term, "row", scatter_dimension=0, tiled=True),
        lax.psum_scatter(up_bias_term, "row", scatter_dimension=0, tiled=True),
        lax.psum_scatter(gain_term, "row", scatter_dimension=0, tiled=True),
        lax.psum_scatter(shift_term, "row", scatter_dimension=0, tiled=True),
    )
    scaled = dnorm * gain
    dconv = inv * (
        scaled
        - jnp.mean(scaled, axis=2, keepdims=True)
        - normed * jnp.mean(scaled * normed, axis=2, keepdims=True)
    )
    dconv = dconv.astype(jnp.bfloat16)
    dconv_wide = dconv.astype(jnp.float32)
    back_rim = with_halo(dconv, (("row", 0),), 3)
    back_pad = jnp.pad(back_rim.astype(jnp.float32), ((0, 0), (3, 3), (0, 0)))
    grad_features = (
        cotangent.astype(jnp.float32) + depth_conv_back(back_pad, kernel, height, width)
    ).astype(jnp.bfloat16)
    taps = []
    for first in range(7):
        for second in range(7):
            taps.append(
                jnp.sum(
                    dconv_wide * padded[first : first + height, second : second + width, :],
                    axis=(0, 1),
                )
            )
    kernel_term = jnp.stack(taps, axis=0) * scale
    conv_bias_term = jnp.sum(dconv_wide, axis=(0, 1)) * scale
    grad_depth_weight, grad_depth_bias = (
        lax.psum_scatter(kernel_term, "row", scatter_dimension=1, tiled=True),
        lax.psum_scatter(conv_bias_term, "row", scatter_dimension=0, tiled=True),
    )
    return (
        block_out,
        grad_features,
        grad_up_weight,
        grad_down_weight,
        grad_depth_weight,
        grad_depth_bias,
        grad_norm_gain,
        grad_norm_shift,
        grad_up_bias,
        grad_down_bias,
    )


def solution(mesh):
    placed = (
        P(("groups", "row"), None, None),
        P(("groups", "row"), None, None),
        P(None, "row"),
        P("row"),
        P("row"),
        P("row"),
        P("row", None),
        P("row"),
        P("row", None),
        P("row"),
    )
    return jax.shard_map(
        per_device,
        mesh=mesh,
        in_specs=placed,
        out_specs=(
            P(("groups", "row"), None, None),
            P(("groups", "row"), None, None),
            P(("groups", "row"), None),
            P(("groups", "row"), None),
            P("groups", "row"),
            P(("groups", "row")),
            P(("groups", "row")),
            P(("groups", "row")),
            P(("groups", "row")),
            P(("groups", "row")),
        ),
        check_vma=False,
    )
```

profile of v0, /device:TPU:0, one launch (start us, length us, event | category | flops | bytes accessed | tf_op | source)
XLA Modules:
  0.0 336.8 jit_solution(5923359344454385601)
XLA Ops:
  7.2 0.0 all-gather.4.cloned.1.call-start
  7.2 0.7 all-gather.4.cloned.1.call-update
  7.9 0.0 all-gather.6.cloned.1.call-start
  8.0 0.7 all-gather.6.cloned.1.call-update
  8.7 0.0 reduce-scatter.10.cloned.1.call-start
  8.7 1.1 fusion.148
  9.8 2.4 collective-permute-start
  12.2 1.3 collective-permute-start.1
  13.5 25.6 %all_gather.26 = bf16[49,512]{0,1:T(8,128)(2,1)S(1)} all-gather(bf16[49,32]{0,1:T(8,128)(2,1)} %param.12), channel_id=1, replica_groups=mesh['groups'=2,'row'=16] {'row'}, dimensions={1}, use_global_device_ids=true | all-gather | bytes 53312 | tf_op jit(solution)/shard_map/all_gather | solution.py:74
  39.1 2.6 slice_reduce_fusion.48
  41.8 0.0 copy-start.62
  41.8 0.0 copy-start.66
  41.8 0.0 copy-start.67
  41.8 1.6 slice_reduce_fusion.46
  43.5 0.6 fusion.149
  44.7 0.2 dynamic-update-slice
  45.0 0.2 dynamic-update-slice.1
  45.2 0.2 dynamic-update-slice.2
  45.5 0.2 dynamic-update-slice.3
  45.7 30.5 %all-reduce.12 = (bf16[512]{0:T(512)(128)(2,1)S(1)}, bf16[512]{0:T(512)(128)(2,1)S(1)}, bf16[512]{0:T(512)(128)(2,1)S(1)}, bf16[512]{0:T(512)(128)(2,1)}) all-reduce(bf16[512]{0:T(512)(128)(2,1)S(1)} %dynamic-update-slice, bf16[512]{0:T(512)(128)(2,1)S(1)} %dynamic-update-slice.2, ...), channel_id=1, replica_groups=mesh['groups'=2,'row'=16] {'row'}, use_global_device_ids=true, to_apply=%add.2 | all-reduce | flops 2048 | bytes 8192
  76.2 17.5 %all-gather = bf16[16,1,128]{2,1,0:T(2,128)(2,1)S(1)} all-gather(bf16[1,1,128]{2,1,0:T(2,128)(2,1)S(1)} %bitcast.131), channel_id=1, replica_groups=mesh['groups'=2,'row'=16] {'row'}, dimensions={0}, use_global_device_ids=true | all-gather | bytes 4352 | tf_op jit(solution)/shard_map/all_gather | solution.py:79
  93.8 2.7 slice_reduce_fusion.47
  96.7 0.1 maximum_convert_fusion
  96.8 4.7 %fusion.146 = (f32[4,64]{1,0:T(4,128)S(1)}, f32[4,64,512]{2,1,0:T(8,128)S(1)}) fusion(f32[512]{0:T(512)S(1)} %convert_element_type.62, f32[512]{0:T(512)S(1)} %get-tuple-element.85, f32[512]{0:T(512)S(1)} %get-tuple-element.86, f32[512]{0:T(512)S(1)} %get-tuple-element.87, f32[512]{0:T(512)S(1)} %get-tuple-element.88, ...), kind=kLoop, calls=%fused_computation.368 | loop fusion | flops 12975872 | bytes 5608448 | tf_op jit(solution)/shard_map/reduce_sum | solution.py:86
  101.7 0.2 multiply_reduce_fusion.3
  101.9 0.2 add_convert_fusion.1
  102.1 0.0 copy-start.2
  102.1 0.0 all-gather.4.cloned.1.call-done
  102.1 3.8 %multiply_convert_fusion = (bf16[256,2048]{1,0:T(8,128)(2,1)S(1)}, f32[256,2048]{1,0:T(8,128)}) fusion(f32[2048]{0:T(1024)S(1)} %bitcast.81, bf16[256,512]{1,0:T(8,128)(2,1)S(1)} %bitcast.75, bf16[512,2048]{1,0:T(8,128)(2,1)} %all-gather.4.cloned.1.call-done), kind=kOutput, calls=%fused_computation.61 | convolution fusion | flops 540016640 | bytes 5513216 | tf_op jit(solution)/shard_map/dot_general | solution.py:95
  106.0 4.2 %convert_reduce_fusion.1 = (f32[2048]{0:T(1024)}, bf16[256,2048]{1,0:T(8,128)(2,1)S(1)}) fusion(f32[256,2048]{1,0:T(8,128)} %get-tuple-element.152, bf16[256,512]{1,0:T(8,128)(2,1)} %bitcast.77, bf16[2048,512]{1,0:T(8,128)(2,1)} %all-gather.6.cloned.1.call-done), kind=kOutput, calls=%fused_computation.60 | convolution fusion | flops 543160320 | bytes 5513216 | tf_op jit(solution)/shard_map/dot_general | solution.py:116
  110.2 1.3 fusion.145
  111.5 0.8 copy-done
  112.3 0.8 multiply_reduce_fusion
  113.1 0.6 broadcast_multiply_fusion.6
  113.7 0.7 div.17
  114.4 3.2 fusion.143
  117.5 1.4 fusion.142
  119.1 0.0 copy-start.3
  119.1 1.0 fusion.144
  120.3 2.3 stack.199
  122.6 0.9 copy.22
  123.5 0.0 reduce-scatter.10.cloned.1.call-update
  123.5 0.3 reduce-scatter.6.cloned.1.call-start
  123.8 3.9 %convolution_multiply_fusion.1 = f32[512,2048]{1,0:T(8,128)} fusion(bf16[256,512]{1,0:T(8,128)(2,1)S(1)} %bitcast.76, bf16[256,2048]{1,0:T(8,128)(2,1)} %copy-done.6), kind=kOutput, calls=%fused_computation.51 | convolution fusion | flops 537919488 | bytes 5505024 | tf_op jit(solution)/shard_map/dot_general | solution.py:125
  127.7 0.0 reduce-scatter.6.cloned.1.call-update
  127.7 0.0 reduce-scatter.8.cloned.1.call-start
  127.7 0.9 copy-done.4
  128.6 2.7 convolution_multiply_fusion
  131.3 0.0 reduce-scatter.8.cloned.1.call-update
  132.7 0.1 convert_reduce_fusion.2
  132.8 59.3 %all-reduce.11 = (f32[512]{0:T(512)S(1)}, f32[512]{0:T(512)S(1)}, f32[512]{0:T(512)S(1)}, f32[2048]{0:T(1024)S(1)}, f32[512]{0:T(512)S(1)}) all-reduce(f32[512]{0:T(512)S(1)} %broadcast_multiply_fusion.5, f32[512]{0:T(512)S(1)} %get-tuple-element.157, ...), channel_id=5, replica_groups=mesh['groups'=2,'row'=16] {'row'}, use_global_device_ids=true, to_apply=%region_57.58.clone | all-reduce | flops 4096 | bytes 32768
  192.1 0.6 dynamic-slice.13
  192.7 0.6 dynamic-slice.9
  193.3 0.6 dynamic-slice.7
  193.9 0.6 dynamic-slice.5
  194.5 1.3 collective-permute-start.2
  195.8 1.3 collective-permute-start.3
  197.1 0.6 dynamic-slice.11
  197.7 2.4 convolution_add_fusion.1
  200.3 0.8 add_convert_fusion
  201.1 0.1 maximum_convert_fusion.1
  201.4 4.7 %fusion.5 = bf16[4,64,512]{2,1,0:T(8,128)(2,1)} fusion(bf16[4,64,512]{2,1,0:T(8,128)(2,1)S(1)} %copy-done.4, f32[10,64,512]{2,1,0:T(8,128)S(1)} %maximum_convert_fusion.1, f32[512]{0:T(512)S(1)} %get-tuple-element.85, f32[512]{0:T(512)S(1)} %get-tuple-element.86, f32[512]{0:T(512)S(1)} %get-tuple-element.87, f32[512]{0:T(512)S(1)} %get-tuple-element.88, ...), kind=kLoop, calls=%fused_computation.152 | loop fusion | flops 13107200 | bytes 5605376 | tf_op jit(solution)/shard_map/convert_element_type | solution.py:162
  206.0 48.2 %reduce-scatter.6.cloned.1.call-done = f32[32,2048]{1,0:T(8,128)} async-done(((f32[512,2048]{1,0:T(8,128)}), f32[32,2048]{1,0:T(8,128)}) %reduce-scatter.6.cloned.1.call-update) | async-done | bytes 262160 | tf_op jit(solution)/shard_map/reduce_scatter | solution.py:124
  254.2 76.1 %reduce-scatter.8.cloned.1.call-done = f32[128,512]{1,0:T(8,128)} async-done(((f32[2048,512]{1,0:T(8,128)}), f32[128,512]{1,0:T(8,128)}) %reduce-scatter.8.cloned.1.call-update) | async-done | bytes 262160 | tf_op jit(solution)/shard_map/reduce_scatter | solution.py:115
  (158 shorter events, 0.4 us)
Async XLA Ops:
  7.2 94.9 %all-gather.4.cloned.1.call-start = ((), (), s32[]{:S(2)}) async-start(), calls=%async_computation.3 | async-start | bytes 2228224 | tf_op jit(solution)/shard_map/all_gather | solution.py:97
  7.9 98.0 %all-gather.6.cloned.1.call-start = ((), (), s32[]{:S(2)}) async-start(), calls=%async_computation.4 | async-start | bytes 2228224 | tf_op jit(solution)/shard_map/all_gather | solution.py:104
  8.7 197.4 %reduce-scatter.10.cloned.1.call-start = ((), (), s32[]{:S(2)}) async-start(), calls=%async_computation.7 | async-start | bytes 278528
  9.8 86.9 %collective-permute-start = (bf16[3,64,512]{2,1,0:T(8,128)(2,1)S(1)}, bf16[3,64,512]{2,1,0:T(8,128)(2,1)S(1)}, u32[]{:S(2)}, u32[]{:S(2)}) collective-permute-start(bf16[3,64,512]{2,1,0:T(8,128)(2,1)S(1)} %get-tuple-element.147), channel_id=1, source_target_pairs={{0,1},{1,2},{2,3},{3,4},{4,5},{5,6},{6,7},{7,8},{8,9},{9,10},{10,1... | collective-permute-start | bytes 589832 | tf_op jit(solution)/shard_map/ppermute | solution.py:15
  12.2 84.5 %collective-permute-start.1 = (bf16[3,64,512]{2,1,0:T(8,128)(2,1)S(1)}, bf16[3,64,512]{2,1,0:T(8,128)(2,1)S(1)}, u32[]{:S(2)}, u32[]{:S(2)}) collective-permute-start(bf16[3,64,512]{2,1,0:T(8,128)(2,1)S(1)} %get-tuple-element.148), channel_id=1, source_target_pairs={{1,0},{2,1},{3,2},{4,3},{5,4},{6,5},{7,6},{8,7},{9,8},{10,9},{11,1... | collective-permute-start | bytes 589832 | tf_op jit(solution)/shard_map/ppermute | solution.py:18
  41.8 1.7 copy-start.62
  41.8 2.9 copy-start.66
  41.8 3.2 copy-start.67
  41.8 3.4 %copy-start.68 = (bf16[32]{0:T(256)(128)(2,1)S(1)}, bf16[32]{0:T(256)(128)(2,1)}, u32[]{:S(2)}) copy-start(bf16[32]{0:T(256)(128)(2,1)} %param.15) | copy-start | bytes 196
  41.8 3.7 %copy-start.69 = (bf16[32]{0:T(256)(128)(2,1)S(1)}, bf16[32]{0:T(256)(128)(2,1)}, u32[]{:S(2)}) copy-start(bf16[32]{0:T(256)(128)(2,1)} %param.19) | copy-start | bytes 196
  41.8 34.4 %copy-start.65 = (bf16[128]{0:T(256)(128)(2,1)S(1)}, bf16[128]{0:T(256)(128)(2,1)}, u32[]{:S(2)}) copy-start(bf16[128]{0:T(256)(128)(2,1)} %param.17) | copy-start | bytes 772
  93.8 2.9 copy-start.1
  96.5 5.0 %copy-start.7 = (f32[512]{0:T(512)}, f32[512]{0:T(512)S(1)}, u32[]{:S(2)}) copy-start(f32[512]{0:T(512)S(1)} %get-tuple-element.104) | copy-start | bytes 6148
  96.5 5.0 %copy-start.9 = (f32[512]{0:T(512)}, f32[512]{0:T(512)S(1)}, u32[]{:S(2)}) copy-start(f32[512]{0:T(512)S(1)} %get-tuple-element.105) | copy-start | bytes 6148
  96.5 5.0 %copy-start.11 = (f32[512]{0:T(512)}, f32[512]{0:T(512)S(1)}, u32[]{:S(2)}) copy-start(f32[512]{0:T(512)S(1)} %get-tuple-element.106) | copy-start | bytes 6148
  96.5 5.0 %copy-start.13 = (f32[512]{0:T(512)}, f32[512]{0:T(512)S(1)}, u32[]{:S(2)}) copy-start(f32[512]{0:T(512)S(1)} %get-tuple-element.107) | copy-start | bytes 6148
  96.5 5.0 %copy-start.15 = (f32[512]{0:T(512)}, f32[512]{0:T(512)S(1)}, u32[]{:S(2)}) copy-start(f32[512]{0:T(512)S(1)} %get-tuple-element.108) | copy-start | bytes 6148
  96.5 5.0 %copy-start.17 = (f32[512]{0:T(512)}, f32[512]{0:T(512)S(1)}, u32[]{:S(2)}) copy-start(f32[512]{0:T(512)S(1)} %get-tuple-element.109) | copy-start | bytes 6148
  96.5 5.0 %copy-start.19 = (f32[512]{0:T(512)}, f32[512]{0:T(512)S(1)}, u32[]{:S(2)}) copy-start(f32[512]{0:T(512)S(1)} %get-tuple-element.110) | copy-start | bytes 6148
  96.5 5.0 %copy-start.21 = (f32[512]{0:T(512)}, f32[512]{0:T(512)S(1)}, u32[]{:S(2)}) copy-start(f32[512]{0:T(512)S(1)} %get-tuple-element.111) | copy-start | bytes 6148
  96.6 5.0 %copy-start.23 = (f32[512]{0:T(512)}, f32[512]{0:T(512)S(1)}, u32[]{:S(2)}) copy-start(f32[512]{0:T(512)S(1)} %get-tuple-element.112) | copy-start | bytes 6148
  96.6 5.0 %copy-start.25 = (f32[512]{0:T(512)}, f32[512]{0:T(512)S(1)}, u32[]{:S(2)}) copy-start(f32[512]{0:T(512)S(1)} %get-tuple-element.113) | copy-start | bytes 6148
  96.6 5.0 %copy-start.27 = (f32[512]{0:T(512)}, f32[512]{0:T(512)S(1)}, u32[]{:S(2)}) copy-start(f32[512]{0:T(512)S(1)} %get-tuple-element.114) | copy-start | bytes 6148
  96.6 5.0 %copy-start.29 = (f32[512]{0:T(512)}, f32[512]{0:T(512)S(1)}, u32[]{:S(2)}) copy-start(f32[512]{0:T(512)S(1)} %get-tuple-element.115) | copy-start | bytes 6148
  96.6 5.0 %copy-start.31 = (f32[512]{0:T(512)}, f32[512]{0:T(512)S(1)}, u32[]{:S(2)}) copy-start(f32[512]{0:T(512)S(1)} %get-tuple-element.116) | copy-start | bytes 6148
  96.6 5.0 %copy-start.33 = (f32[512]{0:T(512)}, f32[512]{0:T(512)S(1)}, u32[]{:S(2)}) copy-start(f32[512]{0:T(512)S(1)} %get-tuple-element.117) | copy-start | bytes 6148
  96.6 5.0 %copy-start.35 = (f32[512]{0:T(512)}, f32[512]{0:T(512)S(1)}, u32[]{:S(2)}) copy-start(f32[512]{0:T(512)S(1)} %get-tuple-element.118) | copy-start | bytes 6148
  96.6 5.0 %copy-start.37 = (f32[512]{0:T(512)}, f32[512]{0:T(512)S(1)}, u32[]{:S(2)}) copy-start(f32[512]{0:T(512)S(1)} %get-tuple-element.119) | copy-start | bytes 6148
  96.6 5.0 %copy-start.39 = (f32[512]{0:T(512)}, f32[512]{0:T(512)S(1)}, u32[]{:S(2)}) copy-start(f32[512]{0:T(512)S(1)} %get-tuple-element.120) | copy-start | bytes 6148
  96.7 5.0 %copy-start.41 = (f32[512]{0:T(512)}, f32[512]{0:T(512)S(1)}, u32[]{:S(2)}) copy-start(f32[512]{0:T(512)S(1)} %get-tuple-element.121) | copy-start | bytes 6148
  102.1 3.9 %copy-start.2 = (bf16[4,64,512]{2,1,0:T(8,128)(2,1)}, bf16[4,64,512]{2,1,0:T(8,128)(2,1)S(1)}, u32[]{:S(2)}) copy-start(bf16[4,64,512]{2,1,0:T(8,128)(2,1)S(1)} %add_convert_fusion.1) | copy-start | bytes 786436
  106.0 4.2 %copy-start.5 = (bf16[512,2048]{1,0:T(8,128)(2,1)S(1)}, bf16[512,2048]{1,0:T(8,128)(2,1)}, u32[]{:S(2)}) copy-start(bf16[512,2048]{1,0:T(8,128)(2,1)} %all-gather.4.cloned.1.call-done) | copy-start | bytes 6291460
  110.2 2.9 copy-start.6
  118.9 1.2 copy-start.43
  118.9 1.2 copy-start.44
  119.0 1.2 copy-start.45
  119.0 1.2 copy-start.46
  119.0 1.2 copy-start.47
  119.0 1.2 copy-start.48
  119.0 1.2 copy-start.49
  119.0 1.2 copy-start.50
  119.0 1.2 copy-start.51
  119.0 1.2 copy-start.52
  119.0 1.2 copy-start.53
  119.0 1.2 copy-start.54
  119.0 1.2 copy-start.55
  119.0 1.2 copy-start.56
  119.0 1.2 copy-start.57
  119.1 1.2 copy-start.58
  119.1 4.7 %copy-start.3 = (bf16[4,64,512]{2,1,0:T(8,128)(2,1)S(1)}, bf16[4,64,512]{2,1,0:T(8,128)(2,1)}, u32[]{:S(2)}) copy-start(bf16[4,64,512]{2,1,0:T(8,128)(2,1)} %copy-done.2) | copy-start | bytes 786436
  123.5 130.7 %reduce-scatter.6.cloned.1.call-start = ((), (), s32[]{:S(2)}) async-start(), calls=%async_computation.5 | async-start | bytes 4456448 | tf_op jit(solution)/shard_map/reduce_scatter | solution.py:124
  127.7 202.6 %reduce-scatter.8.cloned.1.call-start = ((), (), s32[]{:S(2)}) async-start(), calls=%async_computation.6 | async-start | bytes 4456448 | tf_op jit(solution)/shard_map/reduce_scatter | solution.py:115
  131.3 1.3 copy-start.64
  131.3 1.4 copy-start.61
  131.3 1.5 copy-start.59
  131.3 1.5 copy-start.63
  131.3 1.5 copy-start.60
  194.5 6.6 %collective-permute-start.2 = (bf16[3,64,512]{2,1,0:T(8,128)(2,1)S(1)}, bf16[3,64,512]{2,1,0:T(8,128)(2,1)S(1)}, u32[]{:S(2)}, u32[]{:S(2)}) collective-permute-start(bf16[3,64,512]{2,1,0:T(8,128)(2,1)S(1)} %get-tuple-element.145), channel_id=1, source_target_pairs={{0,1},{1,2},{2,3},{3,4},{4,5},{5,6},{6,7},{7,8},{8,9},{9,10},{10,1... | collective-permute-start | bytes 589832 | tf_op jit(solution)/shard_map/ppermute | solution.py:15
  195.8 5.3 %collective-permute-start.3 = (bf16[3,64,512]{2,1,0:T(8,128)(2,1)S(1)}, bf16[3,64,512]{2,1,0:T(8,128)(2,1)S(1)}, u32[]{:S(2)}, u32[]{:S(2)}) collective-permute-start(bf16[3,64,512]{2,1,0:T(8,128)(2,1)S(1)} %get-tuple-element.146), channel_id=1, source_target_pairs={{1,0},{2,1},{3,2},{4,3},{5,4},{6,5},{7,6},{8,7},{9,8},{10,9},{11,1... | collective-permute-start | bytes 589832 | tf_op jit(solution)/shard_map/ppermute | solution.py:18
  200.1 1.1 copy-start.8
  200.1 1.1 copy-start.10
  200.1 1.1 copy-start.12
  200.1 1.1 copy-start.14
  200.1 1.1 copy-start.16
  (15 other events, 15.6 us)
Sparse Core Ops, SparseCore 0:
  10.1 44.2 all-gather.3
  56.6 40.1 all-gather.5
  123.6 54.3 reduce-scatter.9
  182.2 71.8 reduce-scatter.5
  258.4 71.7 reduce-scatter.7
where the time goes:
time: 337 us
  blocking collectives  133 us (39%)
  waiting for transfers between devices  126 us (37%)
  matrix products  18.4 us (5%)
  local copies, waits for them, and re-layouts  18.3 us (5%)
  other arithmetic  17.8 us (5%)
  between operations  16.9 us (5%)
  starting transfers between devices  6.71 us (2%)
    unnamed x2, blocking collectives  89.8 us
    reduce_scatter x1, waiting for transfers between devices, per_device(): lax.psum_scatter(down_full, 'row', scatter_dimension=0, tiled=True)  76.1 us
    reduce_scatter x1, waiting for transfers between devices, per_device(): lax.psum_scatter(lax.dot_general(columns, dhidden, (((0,), (0,)), ((), ()...  48.2 us
    all_gather x1, blocking collectives, per_device(): lax.all_gather(depth_weight, 'row', axis=1, tiled=True)  25.6 us
    all_gather x1, blocking collectives, per_device(): lax.all_gather(up_bias, 'row', axis=0, tiled=True)  17.5 us
    unnamed x155, local copies, waits for them, and re-layouts  7.34 us
    slice x3, local copies, waits for them, and re-layouts, depth_conv(): kernel[first * 7 + second]  6.92 us
  transfers between devices with their start and end apart: 9, of which 2 were waited for; matrix products, arithmetic and copies ran while one was open for 11% of the time, Pallas kernels for 0%

commit v1 on v0

--- a/solution.py
+++ b/solution.py
@@ -5,6 +5,32 @@
 from jax.sharding import PartitionSpec as P
 
 eps = 1e-06
+
+
+def convert_wires_over_axis(matrix, at_axis):
+    wide_out = list(matrix.shape[1:])
+    wide_out[at_axis] *= matrix.shape[0]
+    return jnp.moveaxis(matrix, 0, at_axis).reshape(wide_out)
+
+
+def work_the_tiles(unit, group_axis):
+    part_next = lax.axis_index(group_axis)
+    p_next = lax.axis_size(group_axis)
+    r1, ready = (p_next, part_next)
+    small, y = (unit[None], 1)
+    while y < r1:
+        parts_seen = []
+        ix = 0
+        while ix < r1:
+            parts_seen.append((ix, ix ^ y))
+            ix += 1
+        block_next = lax.ppermute(small, group_axis, parts_seen)
+        even = ready & y == 0
+        tile_out = jnp.where(even, small, block_next)
+        o_now = jnp.where(even, block_next, small)
+        small = jnp.concatenate([tile_out, o_now])
+        y *= 2
+    return small
 
 
 def with_halo(block, sides, width):
@@ -66,12 +92,17 @@
     down_weight,
     down_bias,
 ):
+
+    def advance_sheets(sample, local, axis_k):
+        top = work_the_tiles(sample, local)
+        return convert_wires_over_axis(top, axis_k)
+
     height, width, chans = features.shape
     devices = lax.axis_size("row")
     cells = height * width
     scale = 1.0 / math.sqrt(cells * devices)
     kernel, conv_bias, gain, shift, bias_down, bias_up = (
-        lax.all_gather(depth_weight, "row", axis=1, tiled=True),
+        advance_sheets(depth_weight, "row", 1),
         lax.all_gather(depth_bias, "row", axis=0, tiled=True),
         lax.all_gather(norm_gain, "row", axis=0, tiled=True),
         lax.all_gather(norm_shift, "row", axis=0, tiled=True),

time: 337 us -> 335 us (level)
  blocking collectives: 133 us -> 111 us
  starting transfers between devices: 6.71 us -> 14.1 us
  local copies, waits for them, and re-layouts: 18.3 us -> 25.1 us
  waiting for transfers between devices: 126 us -> 130 us
    all_gather x1 -> x0, blocking collectives: 25.6 us -> none  [per_device(): lax.all_gather(depth_weight, 'row', axis=1, tiled=True)]
    ppermute x0 -> x4, starting transfers between devices: none -> 8.71 us  [work_the_tiles(): block_next = lax.ppermute(small, group_axis, parts_seen)]
    ppermute x0 -> x4, waiting for transfers between devices: none -> 4.46 us  [work_the_tiles(): block_next = lax.ppermute(small, group_axis, parts_seen)]
    mul x0 -> x49, local copies, waits for them, and re-layouts: none -> 3.8 us  [depth_conv(): padded[first:first + height, second:second + width, :]]
    unnamed x2, blocking collectives: 89.8 us -> 93.6 us
    unnamed x155 -> x143, local copies, waits for them, and re-layouts: 7.34 us -> 10.4 us
  transfers between devices with their start and end apart: 9 -> 13, of which waited for: 2 -> 5; matrix products, arithmetic and copies ran while one was open for 11% -> 13% of each run, Pallas kernels for 0% -> 0%
where the time goes in v1:
time: 335 us; the launch traced here: 334 us
  waiting for transfers between devices  130 us (39%)
  blocking collectives  111 us (33%)
  local copies, waits for them, and re-layouts  25.1 us (7%)
  other arithmetic  18.8 us (6%)
  matrix products  18.4 us (5%)
  between operations  16.8 us (5%)
  starting transfers between devices  14.1 us (4%)
    unnamed x2, blocking collectives  93.6 us
    reduce_scatter x1, waiting for transfers between devices, per_device(): lax.psum_scatter(down_full, 'row', scatter_dimension=0, tiled=True)  76.2 us
    reduce_scatter x1, waiting for transfers between devices, per_device(): lax.psum_scatter(lax.dot_general(columns, dhidden, (((0,), (0,)), ((), ()...  48.3 us
    all_gather x1, blocking collectives, per_device(): lax.all_gather(up_bias, 'row', axis=0, tiled=True)  17.3 us
    unnamed x143, local copies, waits for them, and re-layouts  10.4 us
    ppermute x4, starting transfers between devices, work_the_tiles(): block_next = lax.ppermute(small, group_axis, parts_seen)  8.71 us
    slice x3, local copies, waits for them, and re-layouts, depth_conv(): kernel[first * 7 + second]  6.84 us
  transfers between devices with their start and end apart: 13, of which 5 were waited for; matrix products, arithmetic and copies ran while one was open for 13% of the time, Pallas kernels for 0%

profile of v1, /device:TPU:0, one launch (start us, length us, event | category | flops | bytes accessed | tf_op | source)
XLA Modules:
  0.0 333.9 jit_solution(106703681211687526)
XLA Ops:
  7.2 0.7 all-gather.4.cloned.1.call-update
  8.0 0.6 collective-permute-start.2
  8.5 0.1 all-gather.6.cloned.1.call-update
  8.7 0.8 collective-permute-done.2
  9.6 0.7 broadcast_select_fusion.7
  10.3 2.9 collective-permute-start.3
  13.2 1.7 collective-permute-done.3
  14.9 2.1 collective-permute-start.4
  17.1 1.9 collective-permute-done.4
  19.0 3.1 collective-permute-start.5
  22.1 1.0 fusion.148
  23.2 1.3 collective-permute-start
  24.5 1.3 collective-permute-start.1
  25.8 1.3 fusion.149
  27.8 0.9 dynamic-update-slice
  28.6 0.8 dynamic-update-slice.1
  29.5 0.8 dynamic-update-slice.2
  30.3 0.8 dynamic-update-slice.3
  31.2 34.2 %all-reduce.12 = (bf16[512]{0:T(512)(128)(2,1)S(1)}, bf16[512]{0:T(512)(128)(2,1)S(1)}, bf16[512]{0:T(512)(128)(2,1)S(1)}, bf16[512]{0:T(512)(128)(2,1)}) all-reduce(bf16[512]{0:T(512)(128)(2,1)S(1)} %dynamic-update-slice, bf16[512]{0:T(512)(128)(2,1)S(1)} %dynamic-update-slice.2, ...), channel_id=1, replica_groups=mesh['groups'=2,'row'=16] {'row'}, use_global_device_ids=true, to_apply=%add.2 | all-reduce | flops 2048 | bytes 8192
  65.4 17.3 %all-gather = bf16[16,1,128]{2,1,0:T(2,128)(2,1)S(1)} all-gather(bf16[1,1,128]{2,1,0:T(2,128)(2,1)} %bitcast.137), channel_id=1, replica_groups=mesh['groups'=2,'row'=16] {'row'}, dimensions={0}, use_global_device_ids=true | all-gather | bytes 4352 | tf_op jit(solution)/shard_map/all_gather | solution.py:110
  82.8 2.6 slice_reduce_fusion.48
  85.4 2.7 slice_reduce_fusion.47
  88.1 0.1 mul.1051
  90.6 0.1 mul.1180
  90.7 0.1 mul.1183
  90.8 0.1 mul.1186
  90.8 0.1 mul.1189
  90.9 0.1 mul.1192
  91.0 0.1 mul.1195
  91.1 1.6 slice_reduce_fusion.46
  92.7 0.1 mul.1057
  93.6 0.1 maximum_convert_fusion
  93.8 4.9 %fusion.146 = (f32[4,64]{1,0:T(4,128)S(1)}, f32[4,64,512]{2,1,0:T(8,128)S(1)}) fusion(f32[512]{0:T(512)S(1)} %convert_element_type.67, f32[512]{0:T(512)S(1)} %mul.1195, f32[512]{0:T(512)S(1)} %mul.1192, f32[512]{0:T(512)S(1)} %mul.1189, f32[512]{0:T(512)S(1)} %mul.1186, f32[10,64,512]{2,1,0:T(8,128)S(1)} %maximum_convert_fusion, f32[512]{0:T(512)S(1)} %mul.1183, ...), kind=kLoop, calls=%fused_computation.380 | loop fusion | flops 12975872 | bytes 5608448 | tf_op jit(solution)/shard_map/reduce_sum | solution.py:117
  98.8 0.2 multiply_reduce_fusion.3
  99.0 0.2 add_convert_fusion.1
  99.2 3.8 %multiply_convert_fusion = (bf16[256,2048]{1,0:T(8,128)(2,1)S(1)}, f32[256,2048]{1,0:T(8,128)}) fusion(f32[2048]{0:T(1024)S(1)} %bitcast.86, bf16[256,512]{1,0:T(8,128)(2,1)S(1)} %bitcast.80, bf16[512,2048]{1,0:T(8,128)(2,1)} %all-gather.4.cloned.1.call-done), kind=kOutput, calls=%fused_computation.61 | convolution fusion | flops 540016640 | bytes 5513216 | tf_op jit(solution)/shard_map/dot_general | solution.py:126
  103.0 4.2 %convert_reduce_fusion.1 = (f32[2048]{0:T(1024)}, bf16[256,2048]{1,0:T(8,128)(2,1)S(1)}) fusion(f32[256,2048]{1,0:T(8,128)} %get-tuple-element.160, bf16[256,512]{1,0:T(8,128)(2,1)} %bitcast.82, bf16[2048,512]{1,0:T(8,128)(2,1)} %all-gather.6.cloned.1.call-done), kind=kOutput, calls=%fused_computation.60 | convolution fusion | flops 543160320 | bytes 5513216 | tf_op jit(solution)/shard_map/dot_general | solution.py:147
  107.3 1.3 fusion.145
  108.6 0.8 copy-done
  109.4 0.8 multiply_reduce_fusion
  110.2 0.6 broadcast_multiply_fusion.6
  110.8 0.7 div.17
  111.5 3.2 fusion.143
  114.6 1.4 fusion.142
  116.1 1.0 fusion.144
  117.4 2.3 stack.199
  119.7 0.9 copy.22
  120.6 3.9 %convolution_multiply_fusion.1 = f32[512,2048]{1,0:T(8,128)} fusion(bf16[256,512]{1,0:T(8,128)(2,1)S(1)} %bitcast.81, bf16[256,2048]{1,0:T(8,128)(2,1)} %copy-done.6), kind=kOutput, calls=%fused_computation.51 | convolution fusion | flops 537919488 | bytes 5505024 | tf_op jit(solution)/shard_map/dot_general | solution.py:156
  124.6 0.9 copy-done.4
  125.4 2.7 convolution_multiply_fusion
  129.7 59.4 %all-reduce.11 = (f32[512]{0:T(512)S(1)}, f32[512]{0:T(512)S(1)}, f32[512]{0:T(512)S(1)}, f32[2048]{0:T(1024)S(1)}, f32[512]{0:T(512)S(1)}) all-reduce(f32[512]{0:T(512)S(1)} %broadcast_multiply_fusion.5, f32[512]{0:T(512)S(1)} %get-tuple-element.165, ...), channel_id=5, replica_groups=mesh['groups'=2,'row'=16] {'row'}, use_global_device_ids=true, to_apply=%region_57.58.clone | all-reduce | flops 4096 | bytes 32768
  189.0 0.6 dynamic-slice.13
  189.6 0.6 dynamic-slice.9
  190.2 0.6 dynamic-slice.7
  190.8 0.6 dynamic-slice.5
  191.4 1.3 collective-permute-start.6
  192.7 1.3 collective-permute-start.7
  194.0 0.6 dynamic-slice.11
  194.6 2.4 convolution_add_fusion.1
  197.2 0.8 add_convert_fusion
  198.0 0.1 maximum_convert_fusion.1
  198.2 4.7 %fusion.5 = bf16[4,64,512]{2,1,0:T(8,128)(2,1)} fusion(bf16[4,64,512]{2,1,0:T(8,128)(2,1)S(1)} %copy-done.4, f32[10,64,512]{2,1,0:T(8,128)S(1)} %maximum_convert_fusion.1, f32[512]{0:T(512)S(1)} %copy-done.20, f32[512]{0:T(512)S(1)} %copy-done.18, f32[512]{0:T(512)S(1)} %copy-done.16, f32[512]{0:T(512)S(1)} %copy-done.14, f32[512]{0:T(512)S(1)} %copy-done.12, ...), kind=kLoop, calls=%fused_computation.152 | loop fusion | flops 13107200 | bytes 5605376 | tf_op jit(solution)/shard_map/convert_element_type | solution.py:193
  202.9 48.3 %reduce-scatter.6.cloned.1.call-done = f32[32,2048]{1,0:T(8,128)} async-done(((f32[512,2048]{1,0:T(8,128)}), f32[32,2048]{1,0:T(8,128)}) %reduce-scatter.6.cloned.1.call-update) | async-done | bytes 262160 | tf_op jit(solution)/shard_map/reduce_scatter | solution.py:155
  251.2 76.2 %reduce-scatter.8.cloned.1.call-done = f32[128,512]{1,0:T(8,128)} async-done(((f32[2048,512]{1,0:T(8,128)}), f32[128,512]{1,0:T(8,128)}) %reduce-scatter.8.cloned.1.call-update) | async-done | bytes 262160 | tf_op jit(solution)/shard_map/reduce_scatter | solution.py:146
  (209 shorter events, 4.0 us)
Async XLA Ops:
  7.2 92.0 %all-gather.4.cloned.1.call-start = ((), (), s32[]{:S(2)}) async-start(), calls=%async_computation.3 | async-start | bytes 2228224 | tf_op jit(solution)/shard_map/all_gather | solution.py:128
  7.9 95.1 %all-gather.6.cloned.1.call-start = ((), (), s32[]{:S(2)}) async-start(), calls=%async_computation.4 | async-start | bytes 2228224 | tf_op jit(solution)/shard_map/all_gather | solution.py:135
  8.0 1.6 collective-permute-start.2
  8.7 194.2 %reduce-scatter.10.cloned.1.call-start = ((), (), s32[]{:S(2)}) async-start(), calls=%async_computation.7 | async-start | bytes 278528
  10.3 4.6 %collective-permute-start.3 = (bf16[2,49,32]{1,2,0:T(8,128)(2,1)S(1)}, bf16[2,49,32]{1,2,0:T(8,128)(2,1)S(1)}, u32[]{:S(2)}, u32[]{:S(2)}) collective-permute-start(bf16[2,49,32]{1,2,0:T(8,128)(2,1)S(1)} %pad_maximum_fusion.2), channel_id=1, source_target_pairs={{0,2},{1,3},{2,0},{3,1},{4,6},{5,7},{6,4},{7,5},{8,10},{9,11},{10,... | collective-permute-start | bytes 18824 | tf_op jit(solution)/shard_map/ppermute | solution.py:27
  14.9 4.0 %collective-permute-start.4 = (bf16[4,49,32]{1,2,0:T(8,128)(2,1)S(1)}, bf16[4,49,32]{1,2,0:T(8,128)(2,1)S(1)}, u32[]{:S(2)}, u32[]{:S(2)}) collective-permute-start(bf16[4,49,32]{1,2,0:T(8,128)(2,1)S(1)} %pad_maximum_fusion.1), channel_id=1, source_target_pairs={{0,4},{1,5},{2,6},{3,7},{4,0},{5,1},{6,2},{7,3},{8,12},{9,13},{10,... | collective-permute-start | bytes 37640 | tf_op jit(solution)/shard_map/ppermute | solution.py:27
  19.0 63.7 %collective-permute-start.5 = (bf16[8,49,32]{1,2,0:T(8,128)(2,1)S(1)}, bf16[8,49,32]{1,2,0:T(8,128)(2,1)S(1)}, u32[]{:S(2)}, u32[]{:S(2)}) collective-permute-start(bf16[8,49,32]{1,2,0:T(8,128)(2,1)S(1)} %pad_maximum_fusion), channel_id=1, source_target_pairs={{0,8},{1,9},{2,10},{3,11},{4,12},{5,13},{6,14},{7,15},{8,0},{9,1},... | collective-permute-start | bytes 75272 | tf_op jit(solution)/shard_map/ppermute | solution.py:27
  23.2 70.4 %collective-permute-start = (bf16[3,64,512]{2,1,0:T(8,128)(2,1)S(1)}, bf16[3,64,512]{2,1,0:T(8,128)(2,1)S(1)}, u32[]{:S(2)}, u32[]{:S(2)}) collective-permute-start(bf16[3,64,512]{2,1,0:T(8,128)(2,1)S(1)} %get-tuple-element.147), channel_id=1, source_target_pairs={{0,1},{1,2},{2,3},{3,4},{4,5},{5,6},{6,7},{7,8},{8,9},{9,10},{10,1... | collective-permute-start | bytes 589832 | tf_op jit(solution)/shard_map/ppermute | solution.py:41
  24.5 69.1 %collective-permute-start.1 = (bf16[3,64,512]{2,1,0:T(8,128)(2,1)S(1)}, bf16[3,64,512]{2,1,0:T(8,128)(2,1)S(1)}, u32[]{:S(2)}, u32[]{:S(2)}) collective-permute-start(bf16[3,64,512]{2,1,0:T(8,128)(2,1)S(1)} %get-tuple-element.148), channel_id=1, source_target_pairs={{1,0},{2,1},{3,2},{4,3},{5,4},{6,5},{7,6},{8,7},{9,8},{10,9},{11,1... | collective-permute-start | bytes 589832 | tf_op jit(solution)/shard_map/ppermute | solution.py:44
  88.1 5.5 %copy-start.1 = (bf16[4,64,512]{2,1,0:T(8,128)(2,1)S(1)}, bf16[4,64,512]{2,1,0:T(8,128)(2,1)}, u32[]{:S(2)}) copy-start(bf16[4,64,512]{2,1,0:T(8,128)(2,1)} %param.10) | copy-start | bytes 786436
  90.6 3.1 copy-start.7
  90.7 3.0 copy-start.9
  90.8 3.0 copy-start.11
  90.8 2.9 copy-start.13
  90.9 2.8 copy-start.15
  91.0 2.7 copy-start.17
  91.1 2.7 copy-start.19
  92.8 5.9 %copy-start.21 = (f32[512]{0:T(512)}, f32[512]{0:T(512)S(1)}, u32[]{:S(2)}) copy-start(f32[512]{0:T(512)S(1)} %mul.1057) | copy-start | bytes 6148
  92.8 5.8 %copy-start.23 = (f32[512]{0:T(512)}, f32[512]{0:T(512)S(1)}, u32[]{:S(2)}) copy-start(f32[512]{0:T(512)S(1)} %mul.1060) | copy-start | bytes 6148
  92.9 5.8 %copy-start.25 = (f32[512]{0:T(512)}, f32[512]{0:T(512)S(1)}, u32[]{:S(2)}) copy-start(f32[512]{0:T(512)S(1)} %mul.1063) | copy-start | bytes 6148
  93.0 5.7 %copy-start.27 = (f32[512]{0:T(512)}, f32[512]{0:T(512)S(1)}, u32[]{:S(2)}) copy-start(f32[512]{0:T(512)S(1)} %mul.1066) | copy-start | bytes 6148
  93.1 5.6 %copy-start.29 = (f32[512]{0:T(512)}, f32[512]{0:T(512)S(1)}, u32[]{:S(2)}) copy-start(f32[512]{0:T(512)S(1)} %mul.1069) | copy-start | bytes 6148
  93.2 5.5 %copy-start.31 = (f32[512]{0:T(512)}, f32[512]{0:T(512)S(1)}, u32[]{:S(2)}) copy-start(f32[512]{0:T(512)S(1)} %mul.1072) | copy-start | bytes 6148
  93.2 5.5 %copy-start.33 = (f32[512]{0:T(512)}, f32[512]{0:T(512)S(1)}, u32[]{:S(2)}) copy-start(f32[512]{0:T(512)S(1)} %mul.1075) | copy-start | bytes 6148
  93.3 5.4 %copy-start.35 = (f32[512]{0:T(512)}, f32[512]{0:T(512)S(1)}, u32[]{:S(2)}) copy-start(f32[512]{0:T(512)S(1)} %mul.1078) | copy-start | bytes 6148
  93.4 5.3 %copy-start.37 = (f32[512]{0:T(512)}, f32[512]{0:T(512)S(1)}, u32[]{:S(2)}) copy-start(f32[512]{0:T(512)S(1)} %mul.1081) | copy-start | bytes 6148
  93.5 5.3 %copy-start.39 = (f32[512]{0:T(512)}, f32[512]{0:T(512)S(1)}, u32[]{:S(2)}) copy-start(f32[512]{0:T(512)S(1)} %mul.1084) | copy-start | bytes 6148
  93.6 5.2 %copy-start.41 = (f32[512]{0:T(512)}, f32[512]{0:T(512)S(1)}, u32[]{:S(2)}) copy-start(f32[512]{0:T(512)S(1)} %mul.1087) | copy-start | bytes 6148
  99.2 3.9 %copy-start.2 = (bf16[4,64,512]{2,1,0:T(8,128)(2,1)}, bf16[4,64,512]{2,1,0:T(8,128)(2,1)S(1)}, u32[]{:S(2)}) copy-start(bf16[4,64,512]{2,1,0:T(8,128)(2,1)S(1)} %add_convert_fusion.1) | copy-start | bytes 786436
  103.0 4.2 %copy-start.5 = (bf16[512,2048]{1,0:T(8,128)(2,1)S(1)}, bf16[512,2048]{1,0:T(8,128)(2,1)}, u32[]{:S(2)}) copy-start(bf16[512,2048]{1,0:T(8,128)(2,1)} %all-gather.4.cloned.1.call-done) | copy-start | bytes 6291460
  107.3 2.9 copy-start.6
  116.0 1.2 copy-start.43
  116.0 1.2 copy-start.44
  116.0 1.2 copy-start.45
  116.0 1.2 copy-start.46
  116.0 1.2 copy-start.47
  116.0 1.2 copy-start.48
  116.0 1.2 copy-start.49
  116.0 1.2 copy-start.50
  116.1 1.2 copy-start.51
  116.1 1.2 copy-start.52
  116.1 1.2 copy-start.53
  116.1 1.2 copy-start.54
  116.1 1.2 copy-start.55
  116.1 1.2 copy-start.56
  116.1 1.2 copy-start.57
  116.1 1.2 copy-start.58
  116.1 4.5 %copy-start.3 = (bf16[4,64,512]{2,1,0:T(8,128)(2,1)S(1)}, bf16[4,64,512]{2,1,0:T(8,128)(2,1)}, u32[]{:S(2)}) copy-start(bf16[4,64,512]{2,1,0:T(8,128)(2,1)} %copy-done.2) | copy-start | bytes 786436
  120.5 130.7 %reduce-scatter.6.cloned.1.call-start = ((), (), s32[]{:S(2)}) async-start(), calls=%async_computation.5 | async-start | bytes 4456448 | tf_op jit(solution)/shard_map/reduce_scatter | solution.py:155
  124.5 202.8 %reduce-scatter.8.cloned.1.call-start = ((), (), s32[]{:S(2)}) async-start(), calls=%async_computation.6 | async-start | bytes 4456448 | tf_op jit(solution)/shard_map/reduce_scatter | solution.py:146
  128.2 1.3 copy-start.63
  128.2 1.4 copy-start.61
  128.2 1.5 copy-start.59
  128.2 1.5 copy-start.62
  128.2 1.5 copy-start.60
  191.4 6.6 %collective-permute-start.6 = (bf16[3,64,512]{2,1,0:T(8,128)(2,1)S(1)}, bf16[3,64,512]{2,1,0:T(8,128)(2,1)S(1)}, u32[]{:S(2)}, u32[]{:S(2)}) collective-permute-start(bf16[3,64,512]{2,1,0:T(8,128)(2,1)S(1)} %get-tuple-element.145), channel_id=1, source_target_pairs={{0,1},{1,2},{2,3},{3,4},{4,5},{5,6},{6,7},{7,8},{8,9},{9,10},{10,1... | collective-permute-start | bytes 589832 | tf_op jit(solution)/shard_map/ppermute | solution.py:41
  192.7 5.2 %collective-permute-start.7 = (bf16[3,64,512]{2,1,0:T(8,128)(2,1)S(1)}, bf16[3,64,512]{2,1,0:T(8,128)(2,1)S(1)}, u32[]{:S(2)}, u32[]{:S(2)}) collective-permute-start(bf16[3,64,512]{2,1,0:T(8,128)(2,1)S(1)} %get-tuple-element.146), channel_id=1, source_target_pairs={{1,0},{2,1},{3,2},{4,3},{5,4},{6,5},{7,6},{8,7},{9,8},{10,9},{11,1... | collective-permute-start | bytes 589832 | tf_op jit(solution)/shard_map/ppermute | solution.py:44
  197.0 1.1 copy-start.8
  197.0 1.1 copy-start.10
  197.0 1.1 copy-start.12
  197.0 1.1 copy-start.14
  197.0 1.1 copy-start.16
  197.1 1.1 copy-start.18
  197.1 1.1 copy-start.20
  (13 other events, 13.5 us)
Sparse Core Ops, SparseCore 0:
  10.1 45.4 all-gather.3
  57.8 40.3 all-gather.5
  120.7 54.3 reduce-scatter.9
  179.3 71.8 reduce-scatter.5
  255.5 71.8 reduce-scatter.7
